TPU v7x, 256 devices: a whole 4x4x8 slice. The times are simulated.
256 devices in a mesh: level: 4 (over z_hi, core), dom: 64 (over z_lo, x, y).
Axes of the slice: x: 4, y: 4, z: 8 (z_hi: 2, z_lo: 4; z = z_hi * 4 + z_lo), core: 2. Of those that a mesh axis runs over, the one named last changes fastest.
Arguments:
- loads: float32 [4, 64, 131072], P('level', None, 'dom'), may hold values from -6 to 6
- level_blocks: bfloat16 [4, 1024, 12, 128, 128], P('level', 'dom'), may hold values from -0.15625 to 0.15625
- level_cols: int32 [4, 1024, 12], P('level', 'dom'), may hold values from 0 to 27, as said below
- smoother: bfloat16 [4, 1024, 128, 128], P('level', 'dom'), may hold values from -0.375 to 0.375
- transfer_blocks: bfloat16 [4, 1024, 8, 128, 128], P('level', 'dom'), may hold values from -0.1875 to 0.1875
- transfer_cols: int32 [4, 1024, 8], P('level', 'dom'), may hold values from 0 to 15
- bound_rows: int32 [4, 64, 3, 4], P('level', 'dom'), may hold values from 0 to 15, as said below
Outputs:
- final_state: float32 [4, 64, 131072], P('level', None, 'dom')
Inputs may be any that keep to these rules, and one draw needn't show every extreme that they name: `level_cols`: values below 16 name a device's own block rows; 16 + side * 4 + j names entry j of bound_rows[g, d, side]. On sections 2 and 3 a block row below 8 names only own block rows below 8 and entries j < 2; any other block row there names only own block rows from 8 on and entries j >= 2. Each list bound_rows[g, d, side] holds 4 distinct block rows of the device on that side; its first 2 entries lie below 8, the others at or above 8.
All inputs are finite; a program needn't handle non-finite values.
Results may differ from a plain program's by a relative error of at most 0.007.
Values may be sent and summed in bfloat16 or wider, within the bound.
A program may use at most 64 MiB of HBM per device.

v0:
```python
import jax
import jax.numpy as jnp
from jax import lax
from jax.sharding import PartitionSpec as P

ITERS = 2


def partner(x, axis, apart):
    return lax.ppermute(x, axis, [(i, i ^ 1 << apart) for i in range(lax.axis_size(axis))])


def extended_2(block, sides, width):
    for axis, dim in sides:
        count = lax.axis_size(axis)
        forward = [(i, i + 1) for i in range(count - 1)]
        forward.append((count - 1, 0))
        backward = [(target, source) for source, target in forward]
        low = lax.ppermute(
            lax.slice_in_dim(block, block.shape[dim] - width, None, axis=dim), axis, forward
        )
        high = lax.ppermute(lax.slice_in_dim(block, 0, width, axis=dim), axis, backward)
        block = jnp.concatenate([low, block, high], axis=dim)
    return block


def from_behind(x, axis, by):
    size = lax.axis_size(axis)
    pairs = [(i, i + by) for i in range(size) if 0 <= i + by < size]
    return lax.ppermute(x, axis, pairs)


def apply_blocks(panels, columns, blocks):
    rows_here = columns.shape[0]
    per_row = columns.shape[1]
    picked = jnp.take(panels, columns.reshape(-1), axis=1)
    picked = picked.reshape(panels.shape[0], rows_here, per_row, panels.shape[2])
    return jnp.einsum("cskb,skab->csa", picked, blocks, preferred_element_type=jnp.float32)


def smooth(panels, smoother_here):
    return jnp.einsum("csb,sab->csa", panels, smoother_here, preferred_element_type=jnp.float32)


def local(loads, level_blocks, level_cols, smoother, transfer_blocks, transfer_cols, bound_rows):
    block_rows = level_cols.shape[1]
    width_block = level_blocks.shape[-1]
    load_cols = loads.shape[1]
    list_width = bound_rows.shape[-1]
    section_fine = lax.axis_index("level") < 2
    bound_lists = bound_rows[0, 0]
    blocks_here = level_blocks[0]
    smoother_here = smoother[0]
    transfer_here = transfer_blocks[0]
    transfer_pattern = transfer_cols[0]
    load_panels = loads[0].reshape(load_cols, block_rows, width_block)
    sibling_wants = partner(bound_lists[2], "level", 0)
    slot_map = jnp.concatenate(
        [
            block_rows + jnp.arange(block_rows, dtype=jnp.int32),
            bound_lists[0],
            2 * block_rows + bound_lists[1],
            3 * block_rows + jnp.arange(list_width, dtype=jnp.int32),
        ]
    )
    pattern_ext = jnp.take(slot_map, level_cols[0])

    def extend(rounded):
        flat_panels = rounded.reshape(load_cols, block_rows * width_block)
        sibling_pack = jnp.take(rounded, sibling_wants, axis=1).reshape(
            load_cols, list_width * width_block
        )
        from_sibling = partner(sibling_pack, "level", 0)
        beside_all = extended_2(flat_panels, (("dom", 1),), block_rows * width_block)
        joined = jnp.concatenate([beside_all, from_sibling], axis=1)
        return joined.reshape(load_cols, -1, width_block)

    iterate = jnp.zeros((load_cols, block_rows, width_block), jnp.float32)
    residual = load_panels
    correction = iterate
    for cycle_index in range(ITERS):
        if cycle_index > 0:
            extended = extend(iterate.astype(jnp.bfloat16))
            residual = lax.cond(
                section_fine,
                lambda: load_panels - apply_blocks(extended, pattern_ext, blocks_here),
                lambda: load_panels,
            )
        residual_b = residual.astype(jnp.bfloat16)
        arrived = from_behind(residual_b.reshape(load_cols, -1), "level", 2)
        arrived = arrived.reshape(load_cols, block_rows, width_block)
        current = lax.cond(
            section_fine,
            lambda: residual,
            lambda: load_panels + apply_blocks(arrived, transfer_pattern, transfer_here),
        )
        first_step = smooth(current.astype(jnp.bfloat16), smoother_here).astype(jnp.bfloat16)
        applied = apply_blocks(extend(first_step), pattern_ext, blocks_here)
        second_in = (current - applied).astype(jnp.bfloat16)
        correction = first_step.astype(jnp.float32) + smooth(second_in, smoother_here)
        returned = from_behind(correction.astype(jnp.bfloat16).reshape(load_cols, -1), "level", -2)
        returned = returned.reshape(load_cols, block_rows, width_block)
        iterate = lax.cond(
            section_fine,
            lambda: iterate + correction + apply_blocks(returned, transfer_pattern, transfer_here),
            lambda: iterate,
        )
    final_state = jnp.where(section_fine, iterate, correction)
    return final_state.reshape(1, load_cols, block_rows * width_block)


def solution(mesh):
    in_specs = (
        P("level", None, "dom"),
        P("level", "dom", None, None, None),
        P("level", "dom", None),
        P("level", "dom", None, None),
        P("level", "dom", None, None, None),
        P("level", "dom", None),
        P("level", "dom", None, None),
    )
    out_specs = P("level", None, "dom")
    return jax.shard_map(local, mesh=mesh, in_specs=in_specs, out_specs=out_specs, check_vma=False)
```

profile of v0, /device:TPU:64, one launch (start us, length us, event | category | flops | bytes accessed | tf_op | source)
XLA Modules:
  0.0 181.7 jit_solution(15262493631021004183)
XLA Ops:
  1.8 7.3 %collective-permute-start = (bf16[64,2048]{1,0:T(8,128)(2,1)S(1)}, bf16[64,2048]{1,0:T(8,128)(2,1)S(1)}, u32[]{:S(2)}, u32[]{:S(2)}) collective-permute-start(bf16[64,2048]{1,0:T(8,128)(2,1)S(1)} %convert_bitcast_fusion.3), channel_id=1, source_target_pairs={{0,128},{64,192},{1,129},{65,193},{2,130},{66,194},{3,131},{67,195... | collective-permute-start | bytes 786440 | tf_op jit(solution)/shard_map/ppermute | solution.py:30
  13.9 7.0 %collective-permute-done = bf16[64,2048]{1,0:T(8,128)(2,1)S(1)} collective-permute-done((bf16[64,2048]{1,0:T(8,128)(2,1)S(1)}, bf16[64,2048]{1,0:T(8,128)(2,1)S(1)}, u32[]{:S(2)}, u32[]{:S(2)}) %collective-permute-start) | collective-permute-done | bytes 262176 | tf_op jit(solution)/shard_map/ppermute | solution.py:30
  21.5 5.7 %collective-permute-start.2 = (bf16[64,2048]{1,0:T(8,128)(2,1)S(1)}, bf16[64,2048]{1,0:T(8,128)(2,1)S(1)}, u32[]{:S(2)}, u32[]{:S(2)}) collective-permute-start(bf16[64,2048]{1,0:T(8,128)(2,1)S(1)} %copy_bitcast_fusion.12), channel_id=1, source_target_pairs={{1,0},{2,1},{3,2},{4,3},{5,4},{6,5},{7,6},{8,7},{9,8},{10,9},{11,1... | collective-permute-start | bytes 786440 | tf_op jit(solution)/shard_map/ppermute | solution.py:22
  29.2 3.5 %collective-permute-done.2 = bf16[64,2048]{1,0:T(8,128)(2,1)S(1)} collective-permute-done((bf16[64,2048]{1,0:T(8,128)(2,1)S(1)}, bf16[64,2048]{1,0:T(8,128)(2,1)S(1)}, u32[]{:S(2)}, u32[]{:S(2)}) %collective-permute-start.2) | collective-permute-done | bytes 262176 | tf_op jit(solution)/shard_map/ppermute | solution.py:22
  33.4 5.8 %collective-permute-done.1 = bf16[64,2048]{1,0:T(8,128)(2,1)} collective-permute-done((bf16[64,2048]{1,0:T(8,128)(2,1)S(1)}, bf16[64,2048]{1,0:T(8,128)(2,1)}, u32[]{:S(2)}, u32[]{:S(2)}) %collective-permute-start.1) | collective-permute-done | bytes 262176 | tf_op jit(solution)/shard_map/ppermute | solution.py:19
  40.5 2.7 %gather_fusion.7 = bf16[192,64,128]{2,1,0:T(8,128)(2,1)} fusion(bf16[64,52,128]{2,0,1:T(8,128)(2,1)S(1)} %copy_bitcast_fusion.6, s32[1024]{0:T(1024)S(1)} %pad_clamp_fusion.5), kind=kCustom, calls=%fused_computation.8.clone | custom fusion | bytes 6292224 | tf_op jit(solution)/shard_map/jit(_take)/gather | solution.py:36
  43.2 3.4 %broadcast_select_fusion.6 = bf16[192,64,128]{2,1,0:T(8,128)(2,1)} fusion(bf16[192,64,128]{2,1,0:T(8,128)(2,1)} %gather_fusion.7, pred[192]{0:T(512)(128)(4,1)S(1)} %get-tuple-element.255), kind=kLoop, calls=%fused_computation.50 | loop fusion | flops 1572864 | bytes 6291648 | tf_op jit(solution)/shard_map/jit(_take)/select_n | solution.py:36
  46.6 6.3 %fusion.8 = f32[64,16,128]{2,0,1:T(8,128)S(1)} fusion(f32[64,16,128]{2,0,1:T(8,128)S(1)} %get-tuple-element.260, bf16[64,16,12,128]{3,0,2,1:T(8,128)(2,1)} %bitcast.230, bf16[1,16,128,128]{3,2,1,0:T(8,128)(2,1)S(1)} %copy-done, bf16[1,16,12,128,128]{4,3,2,1,0:T(8,128)(2,1)} %param.24, bf16[16,64,128]{2,1,0:T(8,128)(2,1)S(1)} %convolution_convert_fusion.1), kind=kOutput, calls=%fused_computation.57 | convolution fusion | flops 436731904 | bytes 11272192 | tf_op jit(solution)/shard_map/csb,sab->csa/dot_general | solution.py:42
  54.3 27.4 %collective-permute-done.5 = bf16[64,2048]{1,0:T(8,128)(2,1)S(1)} collective-permute-done((bf16[64,2048]{1,0:T(8,128)(2,1)S(1)}, bf16[64,2048]{1,0:T(8,128)(2,1)S(1)}, u32[]{:S(2)}, u32[]{:S(2)}) %collective-permute-start.5) | collective-permute-done | bytes 262176 | tf_op jit(solution)/shard_map/ppermute | solution.py:30
  81.6 6.8 %conditional.14 = (f32[64,16,128]{2,0,1:T(8,128)S(1)}) conditional(s32[]{:T(128)} %convert_element_type.68, () %tuple.74, (s32[1,16,8]{1,2,0:T(8,128)S(1)}, bf16[64,2048]{1,0:T(8,128)(2,1)S(1)}, bf16[16,8,128,128]{3,2,1,0:T(8,128)(2,1)}, f32[64,16,128]{2,0,1:T(8,128)S(1)}) %tuple.120), branch_computations={%region_2.6_spmd, %region_3.7_spmd} | conditional | flops 269617280 | bytes 33039140 | solution.py:103
  81.9 2.2 %gather_fusion.1 = bf16[128,64,128]{2,1,0:T(8,128)(2,1)} fusion(bf16[64,16,128]{2,0,1:T(8,128)(2,1)S(1)} %copy_bitcast_fusion.1, s32[1024]{0:T(1024)S(1)} %pad_clamp_fusion.1), kind=kCustom, calls=%fused_computation.3.clone | custom fusion | bytes 4194816 | tf_op jit(solution)/shard_map/cond/branch_1_fun/jit(_take)/gather | solution.py:36
  84.1 2.0 %broadcast_select_fusion.1 = bf16[128,64,128]{2,1,0:T(8,128)(2,1)S(1)} fusion(bf16[128,64,128]{2,1,0:T(8,128)(2,1)} %gather_fusion.1, pred[128]{0:T(512)(128)(4,1)S(1)} %compare_and_fusion.1), kind=kLoop, calls=%fused_computation.18 | loop fusion | flops 1048576 | bytes 4194432 | tf_op jit(solution)/shard_map/cond/branch_1_fun/jit(_take)/select_n | solution.py:36
  86.9 1.6 fusion.1
  88.6 2.0 %collective-permute-start.6 = (bf16[64,2048]{1,0:T(8,128)(2,1)S(1)}, bf16[64,2048]{1,0:T(8,128)(2,1)S(1)}, u32[]{:S(2)}, u32[]{:S(2)}) collective-permute-start(bf16[64,2048]{1,0:T(8,128)(2,1)S(1)} %copy_bitcast_fusion.10), channel_id=1, source_target_pairs={{0,1},{1,2},{2,3},{3,4},{4,5},{5,6},{6,7},{7,8},{8,9},{9,10},{10,1... | collective-permute-start | bytes 786440 | tf_op jit(solution)/shard_map/ppermute | solution.py:19
  92.8 3.9 %collective-permute-done.7 = bf16[64,2048]{1,0:T(8,128)(2,1)S(1)} collective-permute-done((bf16[64,2048]{1,0:T(8,128)(2,1)S(1)}, bf16[64,2048]{1,0:T(8,128)(2,1)S(1)}, u32[]{:S(2)}, u32[]{:S(2)}) %collective-permute-start.7) | collective-permute-done | bytes 262176 | tf_op jit(solution)/shard_map/ppermute | solution.py:22
  96.8 9.9 %collective-permute-done.6 = bf16[64,2048]{1,0:T(8,128)(2,1)S(1)} collective-permute-done((bf16[64,2048]{1,0:T(8,128)(2,1)S(1)}, bf16[64,2048]{1,0:T(8,128)(2,1)S(1)}, u32[]{:S(2)}, u32[]{:S(2)}) %collective-permute-start.6) | collective-permute-done | bytes 262176 | tf_op jit(solution)/shard_map/ppermute | solution.py:19
  107.6 10.3 %conditional.15 = (f32[64,16,128]{2,0,1:T(8,128)S(1)}) conditional(s32[]{:T(128)} %convert_element_type.68, f32[64,16,128]{2,0,1:T(8,128)S(1)} %copy.53, (s32[16,12]{1,0:T(8,128)S(1)}, bf16[64,6656]{1,0:T(8,128)(2,1)}, bf16[16,12,128,128]{3,2,1,0:T(8,128)(2,1)}, f32[64,16,128]{2,1,0:T(8,128)S(1)}, s32[192]{0:T(256)S(1)}, /*index=5*/s32[]{:T(128)}, ...), branch_computations={%region_4.8_spmd, %region_5.9_spmd.clone} | conditional | flops 404361216 | bytes 49954480 | solution.py:84
  109.3 2.7 %gather_fusion.4 = bf16[192,64,128]{2,1,0:T(8,128)(2,1)} fusion(bf16[64,52,128]{2,0,1:T(8,128)(2,1)S(1)} %copy_bitcast_fusion.4, s32[1024]{0:T(1024)S(1)} %pad_clamp_fusion.4), kind=kCustom, calls=%fused_computation.2.clone.clone | custom fusion | bytes 6292224 | tf_op jit(solution)/shard_map/cond/branch_1_fun/jit(_take)/gather | solution.py:36
  112.0 2.4 %broadcast_select_fusion.4 = bf16[192,64,128]{2,1,0:T(8,128)(2,1)S(1)} fusion(bf16[192,64,128]{2,1,0:T(8,128)(2,1)} %gather_fusion.4, pred[192]{0:T(512)(128)(4,1)S(1)} %compare_and_fusion.5), kind=kLoop, calls=%fused_computation.39 | loop fusion | flops 1572864 | bytes 6291648 | tf_op jit(solution)/shard_map/cond/branch_1_fun/jit(_take)/select_n | solution.py:36
  115.7 2.3 %fusion.4 = f32[64,16,128]{2,0,1:T(8,128)S(1)} fusion(bf16[64,16,12,128]{3,0,2,1:T(8,128)(2,1)S(1)} %bitcast.231, bf16[16,12,128,128]{3,2,1,0:T(8,128)(2,1)S(1)} %copy-done.5, f32[64,16,128]{2,1,0:T(8,128)S(1)} %get-tuple-element.234), kind=kOutput, calls=%fused_computation.41 | convolution fusion | flops 402784256 | bytes 10485760 | tf_op jit(solution)/shard_map/cond/branch_1_fun/cskb,skab->csa/dot_general | solution.py:38
  119.3 5.4 %collective-permute-done.9 = bf16[64,2048]{1,0:T(8,128)(2,1)S(1)} collective-permute-done((bf16[64,2048]{1,0:T(8,128)(2,1)S(1)}, bf16[64,2048]{1,0:T(8,128)(2,1)S(1)}, u32[]{:S(2)}, u32[]{:S(2)}) %collective-permute-start.9) | collective-permute-done | bytes 262176 | tf_op jit(solution)/shard_map/ppermute | solution.py:30
  125.2 4.9 %collective-permute-start.11 = (bf16[64,2048]{1,0:T(8,128)(2,1)S(1)}, bf16[64,2048]{1,0:T(8,128)(2,1)S(1)}, u32[]{:S(2)}, u32[]{:S(2)}) collective-permute-start(bf16[64,2048]{1,0:T(8,128)(2,1)S(1)} %copy_bitcast_fusion.8), channel_id=1, source_target_pairs={{1,0},{2,1},{3,2},{4,3},{5,4},{6,5},{7,6},{8,7},{9,8},{10,9},{11,1... | collective-permute-start | bytes 786440 | tf_op jit(solution)/shard_map/ppermute | solution.py:22
  132.1 2.2 %collective-permute-done.11 = bf16[64,2048]{1,0:T(8,128)(2,1)S(1)} collective-permute-done((bf16[64,2048]{1,0:T(8,128)(2,1)S(1)}, bf16[64,2048]{1,0:T(8,128)(2,1)S(1)}, u32[]{:S(2)}, u32[]{:S(2)}) %collective-permute-start.11) | collective-permute-done | bytes 262176 | tf_op jit(solution)/shard_map/ppermute | solution.py:22
  134.2 6.6 %collective-permute-done.10 = bf16[64,2048]{1,0:T(8,128)(2,1)} collective-permute-done((bf16[64,2048]{1,0:T(8,128)(2,1)S(1)}, bf16[64,2048]{1,0:T(8,128)(2,1)}, u32[]{:S(2)}, u32[]{:S(2)}) %collective-permute-start.10) | collective-permute-done | bytes 262176 | tf_op jit(solution)/shard_map/ppermute | solution.py:19
  142.0 2.7 %gather_fusion.10 = bf16[192,64,128]{2,1,0:T(8,128)(2,1)} fusion(bf16[64,52,128]{2,0,1:T(8,128)(2,1)S(1)} %copy_bitcast_fusion.5, s32[1024]{0:T(1024)S(1)} %pad_clamp_fusion.5), kind=kCustom, calls=%fused_computation.9.clone | custom fusion | bytes 6292224 | tf_op jit(solution)/shard_map/jit(_take)/gather | solution.py:36
  144.7 3.4 %broadcast_select_fusion.5 = bf16[192,64,128]{2,1,0:T(8,128)(2,1)} fusion(bf16[192,64,128]{2,1,0:T(8,128)(2,1)} %gather_fusion.10, pred[192]{0:T(512)(128)(4,1)S(1)} %get-tuple-element.255), kind=kLoop, calls=%fused_computation.49 | loop fusion | flops 1572864 | bytes 6291648 | tf_op jit(solution)/shard_map/jit(_take)/select_n | solution.py:36
  148.1 6.3 %fusion.9 = f32[64,16,128]{2,0,1:T(8,128)S(1)} fusion(f32[64,16,128]{2,0,1:T(8,128)S(1)} %get-tuple-element.263, bf16[64,16,12,128]{3,0,2,1:T(8,128)(2,1)} %bitcast.229, bf16[1,16,128,128]{3,2,1,0:T(8,128)(2,1)S(1)} %copy-done, bf16[16,64,128]{2,1,0:T(8,128)(2,1)S(1)} %convolution_convert_fusion, bf16[1,16,12,128,128]{4,3,2,1,0:T(8,128)(2,1)} %param.24), kind=kOutput, calls=%fused_computation.58 | convolution fusion | flops 436731904 | bytes 11272192 | tf_op jit(solution)/shard_map/csb,sab->csa/dot_general | solution.py:42
  155.7 17.9 %collective-permute-done.13 = bf16[64,2048]{1,0:T(8,128)(2,1)S(1)} collective-permute-done((bf16[64,2048]{1,0:T(8,128)(2,1)S(1)}, bf16[64,2048]{1,0:T(8,128)(2,1)S(1)}, u32[]{:S(2)}, u32[]{:S(2)}) %collective-permute-start.13) | collective-permute-done | bytes 262176 | tf_op jit(solution)/shard_map/ppermute | solution.py:30
  173.6 6.8 %conditional.17 = (f32[64,16,128]{2,0,1:T(8,128)S(1)}) conditional(s32[]{:T(128)} %convert_element_type.68, f32[64,16,128]{2,0,1:T(8,128)S(1)} %get-tuple-element.261, (f32[64,16,128]{2,0,1:T(8,128)S(1)}, f32[64,16,128]{2,0,1:T(8,128)S(1)}, bf16[64,2048]{1,0:T(8,128)(2,1)S(1)}, s32[1,16,8]{1,2,0:T(8,128)S(1)}, ...), branch_computations={%region_8.12_spmd, %region_9.13_spmd} | conditional | flops 269748352 | bytes 33563428 | solution.py:103
  173.9 2.2 %gather_fusion.3 = bf16[128,64,128]{2,1,0:T(8,128)(2,1)} fusion(bf16[64,16,128]{2,0,1:T(8,128)(2,1)S(1)} %copy_bitcast_fusion.3, s32[1024]{0:T(1024)S(1)} %pad_clamp_fusion.3), kind=kCustom, calls=%fused_computation.5.clone | custom fusion | bytes 4194816 | tf_op jit(solution)/shard_map/cond/branch_1_fun/jit(_take)/gather | solution.py:36
  176.0 2.0 %broadcast_select_fusion.3 = bf16[128,64,128]{2,1,0:T(8,128)(2,1)S(1)} fusion(bf16[128,64,128]{2,1,0:T(8,128)(2,1)} %gather_fusion.3, pred[128]{0:T(512)(128)(4,1)S(1)} %compare_and_fusion.3), kind=kLoop, calls=%fused_computation.32 | loop fusion | flops 1048576 | bytes 4194432 | tf_op jit(solution)/shard_map/cond/branch_1_fun/jit(_take)/select_n | solution.py:36
  178.9 1.6 fusion.3
  (89 shorter events, 28.1 us)
Async XLA Ops:
  0.0 21.0 %copy-start = (bf16[1,16,128,128]{3,2,1,0:T(8,128)(2,1)S(1)}, bf16[1,16,128,128]{3,2,1,0:T(8,128)(2,1)}, u32[]{:S(2)}) copy-start(bf16[1,16,128,128]{3,2,1,0:T(8,128)(2,1)} %param.26) | copy-start | bytes 1572868
  0.8 13.1 %collective-permute-start.3 = (s32[4]{0:T(128)S(1)}, s32[4]{0:T(128)S(1)}, u32[]{:S(2)}, u32[]{:S(2)}) collective-permute-start(s32[4]{0:T(128)S(1)} %get-tuple-element.258), channel_id=1, source_target_pairs={{0,64},{64,0},{128,192},{192,128},{1,65},{65,1},{129,193},{193,129... | collective-permute-start | bytes 56 | tf_op jit(solution)/shard_map/ppermute | solution.py:10
  1.8 19.1 %collective-permute-start = (bf16[64,2048]{1,0:T(8,128)(2,1)S(1)}, bf16[64,2048]{1,0:T(8,128)(2,1)S(1)}, u32[]{:S(2)}, u32[]{:S(2)}) collective-permute-start(bf16[64,2048]{1,0:T(8,128)(2,1)S(1)} %convert_bitcast_fusion.3), channel_id=1, source_target_pairs={{0,128},{64,192},{1,129},{65,193},{2,130},{66,194},{3,131},{67,195... | collective-permute-start | bytes 786440 | tf_op jit(solution)/shard_map/ppermute | solution.py:30
  12.3 8.7 %copy-start.7 = (s32[1,16,8]{1,2,0:T(8,128)S(1)}, s32[1,16,8]{1,2,0:T(8,128)}, u32[]{:S(2)}) copy-start(s32[1,16,8]{1,2,0:T(8,128)} %param.28) | copy-start | bytes 1540
  21.5 11.2 %collective-permute-start.2 = (bf16[64,2048]{1,0:T(8,128)(2,1)S(1)}, bf16[64,2048]{1,0:T(8,128)(2,1)S(1)}, u32[]{:S(2)}, u32[]{:S(2)}) collective-permute-start(bf16[64,2048]{1,0:T(8,128)(2,1)S(1)} %copy_bitcast_fusion.12), channel_id=1, source_target_pairs={{1,0},{2,1},{3,2},{4,3},{5,4},{6,5},{7,6},{8,7},{9,8},{10,9},{11,1... | collective-permute-start | bytes 786440 | tf_op jit(solution)/shard_map/ppermute | solution.py:22
  27.3 12.0 %collective-permute-start.1 = (bf16[64,2048]{1,0:T(8,128)(2,1)S(1)}, bf16[64,2048]{1,0:T(8,128)(2,1)}, u32[]{:S(2)}, u32[]{:S(2)}) collective-permute-start(bf16[64,2048]{1,0:T(8,128)(2,1)S(1)} %copy_bitcast_fusion.12), channel_id=1, source_target_pairs={{0,1},{1,2},{2,3},{3,4},{4,5},{5,6},{6,7},{7,8},{8,9},{9,10},{10,1... | collective-permute-start | bytes 786440 | tf_op jit(solution)/shard_map/ppermute | solution.py:19
  27.9 1.3 collective-permute-start.4
  32.7 0.7 copy-start.6
  53.0 28.7 %collective-permute-start.5 = (bf16[64,2048]{1,0:T(8,128)(2,1)S(1)}, bf16[64,2048]{1,0:T(8,128)(2,1)S(1)}, u32[]{:S(2)}, u32[]{:S(2)}) collective-permute-start(bf16[64,2048]{1,0:T(8,128)(2,1)S(1)} %copy_bitcast_fusion.11), channel_id=1, source_target_pairs={{128,0},{192,64},{129,1},{193,65},{130,2},{194,66},{131,3},{195,67... | collective-permute-start | bytes 786440 | tf_op jit(solution)/shard_map/ppermute | solution.py:30
  84.1 2.8 %copy-start.2 = (bf16[16,8,128,128]{3,2,1,0:T(8,128)(2,1)S(1)}, bf16[16,8,128,128]{3,2,1,0:T(8,128)(2,1)}, u32[]{:S(2)}) copy-start(bf16[16,8,128,128]{3,2,1,0:T(8,128)(2,1)} %get-tuple-element.125) | copy-start | bytes 12582916 | tf_op jit(solution)/shard_map/cond
  88.6 8.2 %collective-permute-start.7 = (bf16[64,2048]{1,0:T(8,128)(2,1)S(1)}, bf16[64,2048]{1,0:T(8,128)(2,1)S(1)}, u32[]{:S(2)}, u32[]{:S(2)}) collective-permute-start(bf16[64,2048]{1,0:T(8,128)(2,1)S(1)} %copy_bitcast_fusion.10), channel_id=1, source_target_pairs={{1,0},{2,1},{3,2},{4,3},{5,4},{6,5},{7,6},{8,7},{9,8},{10,9},{11,1... | collective-permute-start | bytes 786440 | tf_op jit(solution)/shard_map/ppermute | solution.py:22
  88.6 18.0 %collective-permute-start.6 = (bf16[64,2048]{1,0:T(8,128)(2,1)S(1)}, bf16[64,2048]{1,0:T(8,128)(2,1)S(1)}, u32[]{:S(2)}, u32[]{:S(2)}) collective-permute-start(bf16[64,2048]{1,0:T(8,128)(2,1)S(1)} %copy_bitcast_fusion.10), channel_id=1, source_target_pairs={{0,1},{1,2},{2,3},{3,4},{4,5},{5,6},{6,7},{7,8},{8,9},{9,10},{10,1... | collective-permute-start | bytes 786440 | tf_op jit(solution)/shard_map/ppermute | solution.py:19
  91.3 1.5 collective-permute-start.8
  112.0 3.7 %copy-start.5 = (bf16[16,12,128,128]{3,2,1,0:T(8,128)(2,1)S(1)}, bf16[16,12,128,128]{3,2,1,0:T(8,128)(2,1)}, u32[]{:S(2)}) copy-start(bf16[16,12,128,128]{3,2,1,0:T(8,128)(2,1)} %get-tuple-element.233) | copy-start | bytes 18874372 | tf_op jit(solution)/shard_map/cond
  118.0 6.7 %collective-permute-start.9 = (bf16[64,2048]{1,0:T(8,128)(2,1)S(1)}, bf16[64,2048]{1,0:T(8,128)(2,1)S(1)}, u32[]{:S(2)}, u32[]{:S(2)}) collective-permute-start(bf16[64,2048]{1,0:T(8,128)(2,1)S(1)} %copy_bitcast_fusion.9), channel_id=1, source_target_pairs={{0,128},{64,192},{1,129},{65,193},{2,130},{66,194},{3,131},{67,195... | collective-permute-start | bytes 786440 | tf_op jit(solution)/shard_map/ppermute | solution.py:30
  125.2 9.1 %collective-permute-start.11 = (bf16[64,2048]{1,0:T(8,128)(2,1)S(1)}, bf16[64,2048]{1,0:T(8,128)(2,1)S(1)}, u32[]{:S(2)}, u32[]{:S(2)}) collective-permute-start(bf16[64,2048]{1,0:T(8,128)(2,1)S(1)} %copy_bitcast_fusion.8), channel_id=1, source_target_pairs={{1,0},{2,1},{3,2},{4,3},{5,4},{6,5},{7,6},{8,7},{9,8},{10,9},{11,1... | collective-permute-start | bytes 786440 | tf_op jit(solution)/shard_map/ppermute | solution.py:22
  130.1 10.7 %collective-permute-start.10 = (bf16[64,2048]{1,0:T(8,128)(2,1)S(1)}, bf16[64,2048]{1,0:T(8,128)(2,1)}, u32[]{:S(2)}, u32[]{:S(2)}) collective-permute-start(bf16[64,2048]{1,0:T(8,128)(2,1)S(1)} %copy_bitcast_fusion.8), channel_id=1, source_target_pairs={{0,1},{1,2},{2,3},{3,4},{4,5},{5,6},{6,7},{7,8},{8,9},{9,10},{10,1... | collective-permute-start | bytes 786440 | tf_op jit(solution)/shard_map/ppermute | solution.py:19
  130.7 1.3 collective-permute-start.12
  154.4 19.2 %collective-permute-start.13 = (bf16[64,2048]{1,0:T(8,128)(2,1)S(1)}, bf16[64,2048]{1,0:T(8,128)(2,1)S(1)}, u32[]{:S(2)}, u32[]{:S(2)}) collective-permute-start(bf16[64,2048]{1,0:T(8,128)(2,1)S(1)} %copy_bitcast_fusion.7), channel_id=1, source_target_pairs={{128,0},{192,64},{129,1},{193,65},{130,2},{194,66},{131,3},{195,67... | collective-permute-start | bytes 786440 | tf_op jit(solution)/shard_map/ppermute | solution.py:30
  176.0 2.8 %copy-start.4 = (bf16[16,8,128,128]{3,2,1,0:T(8,128)(2,1)S(1)}, bf16[16,8,128,128]{3,2,1,0:T(8,128)(2,1)}, u32[]{:S(2)}) copy-start(bf16[16,8,128,128]{3,2,1,0:T(8,128)(2,1)} %get-tuple-element.138) | copy-start | bytes 12582916 | tf_op jit(solution)/shard_map/cond
where the time goes:
time: 182 us
  waiting for transfers between devices  93.2 us (51%)
  local copies, waits for them, and re-layouts  24.9 us (14%)
  starting transfers between devices  24.4 us (13%)
  other arithmetic  19.8 us (11%)
  matrix products  19 us (10%)
    ppermute x4, waiting for transfers between devices, from_behind(): return lax.ppermute(x, axis, pairs)  57.6 us
    ppermute x3, waiting for transfers between devices, extended_2(): lax.ppermute(lax.slice_in_dim(block, block.shape[dim] - width, None, axis...  22.3 us
    dot_general x4, matrix products, smooth(): jnp.einsum('csb,sab->csa', panels, smoother_here, preferred_element_type=...  13.6 us
    select_n x8, other arithmetic, apply_blocks(): picked = jnp.take(panels, columns.reshape(-1), axis=1)  13.3 us
    gather x5, local copies, waits for them, and re-layouts, apply_blocks(): picked = jnp.take(panels, columns.reshape(-1), axis=1)  12.4 us
    ppermute x4, starting transfers between devices, from_behind(): return lax.ppermute(x, axis, pairs)  11.2 us
    ppermute x3, starting transfers between devices, extended_2(): lax.ppermute(lax.slice_in_dim(block, 0, width, axis=dim), axis, backward)  10.7 us
    ppermute x3, waiting for transfers between devices, extended_2(): lax.ppermute(lax.slice_in_dim(block, 0, width, axis=dim), axis, backward)  9.56 us
  transfers between devices with their start and end apart: 14, of which 13 were waited for; matrix products, arithmetic and copies ran while one was open for 4% of the time, Pallas kernels for 0%

commit v1 on v0

v1 whole, which is shorter than its diff:
```python
import functools

import jax
import jax.numpy as jnp
from jax import lax
from jax.experimental import pallas as pl
from jax.experimental.pallas import tpu as pltpu
from jax.sharding import PartitionSpec as P

S = 16
BS = 128
K = 12
KT = 8
HB = 4
NCOL = 64
C = 2
M = NCOL // C
U = 4
PIECE = 4
NP = S // PIECE
EXT = S + 3 * HB

BF = jnp.bfloat16
F32 = jnp.float32


def dot(a, b):
    return lax.dot_general(a, b, (((1,), (0,)), ((), ())), preferred_element_type=F32)


def gathered(ref, cols_ref, i, count):
    return jnp.concatenate([ref[cols_ref[0, i, k]] for k in range(count)], axis=1)


def over_rows(body, step=U):
    def group(j, carry):
        for u in range(step):
            body(j * step + u)
        return carry

    lax.fori_loop(0, S // step, group, 0)


def panel_at(i):
    return pl.ds(pl.multiple_of(i * BS, BS), BS)


def kernel(
    loads, level, level_cols, smoother, transfer, transfer_cols, bounds, out,
    level_raw, transfer_raw, smoother_raw, level_t, transfer_t, smoother_t,
    lists, wants,
    load_sem, level_sem, transfer_sem, smoother_sem, list_sem,
    list_send, list_recv, pair_send, pair_recv, ext_send, ext_recv,
    *refs,
):
    refs = list(refs)

    def take(*dims):
        if not dims:
            return refs.pop(0)
        return [take(*dims[1:]) for _ in range(dims[0])]

    load_v = take(C)
    current = take(C)
    corr = take(C)
    state = take(C)
    outgoing = take(2, C)
    arrived = take(2, C)
    own = take(3, C)
    ext = take(3, C)
    pack = take(3, C)

    lv = lax.axis_index("level")
    dm = lax.axis_index("dom")
    doms = lax.axis_size("dom")
    fine = lv < 2
    coarse = lv >= 2
    pair = (lax.rem(lv + 2, 4), dm)
    left = (lv, lax.rem(dm + doms - 1, doms))
    right = (lv, lax.rem(dm + 1, doms))
    sibling = (lv + 1 - 2 * lax.rem(lv, 2), dm)
    mesh_ids = pl.DeviceIdType.MESH

    def load_copy(q):
        return pltpu.make_async_copy(loads.at[0, pl.ds(q * M, M)], load_v[q], load_sem.at[q])

    def level_copy(p):
        rows = pl.ds(p * PIECE, PIECE)
        return pltpu.make_async_copy(level.at[0, rows], level_raw.at[rows], level_sem.at[p])

    def transfer_copy(p):
        rows = pl.ds(p * PIECE, PIECE)
        return pltpu.make_async_copy(transfer.at[0, rows], transfer_raw.at[rows], transfer_sem.at[p])

    smoother_copy = pltpu.make_async_copy(smoother.at[0], smoother_raw, smoother_sem)
    list_copy = pltpu.make_async_copy(bounds.at[0, 0], lists, list_sem)

    def list_out(side):
        target, slot = ((left, 1), (right, 0), (sibling, 2))[side]
        return pltpu.make_async_remote_copy(
            src_ref=lists, dst_ref=wants.at[slot], send_sem=list_send.at[side],
            recv_sem=list_recv.at[slot], device_id=target, device_id_type=mesh_ids)

    def pair_out(t, q):
        return pltpu.make_async_remote_copy(
            src_ref=outgoing[t][q], dst_ref=arrived[t][q], send_sem=pair_send.at[t, q],
            recv_sem=pair_recv.at[t, q], device_id=pair, device_id_type=mesh_ids)

    def ext_out(p, q, side):
        target, slot = ((left, 1), (right, 0), (sibling, 2))[side]
        return pltpu.make_async_remote_copy(
            src_ref=pack[p][q].at[side], dst_ref=ext[p][q].at[pl.ds(S + slot * HB, HB)],
            send_sem=ext_send.at[p, q, side], recv_sem=ext_recv.at[p, q, slot],
            device_id=target, device_id_type=mesh_ids)

    def ext_in(p, q, slot):
        return ext_out(p, q, (1, 0, 2)[slot])

    def exchange(p, q):
        for side in (0, 1, 2):
            entry = (1, 0, 2)[side]
            for j in range(HB):
                pack[p][q][side, j] = own[p][q][wants[side, entry, j]]
            ext_out(p, q, side).start()

    def exchange_wait(p, q):
        for slot in range(3):
            ext_in(p, q, slot).wait_recv()

    def transpose_level():
        for p in range(NP):
            level_copy(p).wait()

            def body(j, carry):
                i = p * PIECE + j
                for k in range(K):
                    level_t[i, k * BS : (k + 1) * BS] = level_raw[i, k].T
                return carry

            lax.fori_loop(0, PIECE, body, 0)

    def transpose_transfer():
        for p in range(NP):
            transfer_copy(p).wait()

            def body(j, carry):
                i = p * PIECE + j
                for k in range(KT):
                    transfer_t[i, k * BS : (k + 1) * BS] = transfer_raw[i, k].T
                return carry

            lax.fori_loop(0, PIECE, body, 0)

    def transpose_smoother():
        smoother_copy.wait()

        def body(i, carry):
            smoother_t[i] = smoother_raw[i].T
            return carry

        lax.fori_loop(0, S, body, 0)

    def keep_step(p, q, i, first):
        own[p][q][i] = first
        ext[p][q][i] = first

    def smooth_rows(p, q, source):
        def body(i):
            keep_step(p, q, i, dot(source[i], smoother_t[i]).astype(BF))

        over_rows(body)

    def restrict_rows(t, p, q):
        def body(i):
            v = load_v[q][:, panel_at(i)] + dot(
                gathered(arrived[t][q], transfer_cols, i, KT), transfer_t[i])
            current[q][i] = v
            keep_step(p, q, i, dot(v.astype(BF), smoother_t[i]).astype(BF))

        over_rows(body)

    def second_step(p, q, give):
        def body(i):
            applied = dot(gathered(ext[p][q], level_cols, i, K), level_t[i])
            second_in = (current[q][i] - applied).astype(BF)
            give(i, own[p][q][i].astype(F32) + dot(second_in, smoother_t[i]))

        over_rows(body)

    def put(q, i, value):
        out[0, q * M : (q + 1) * M, panel_at(i)] = value

    barrier = pltpu.get_barrier_semaphore()
    for target in (left, right, sibling, pair):
        pl.semaphore_signal(barrier, inc=1, device_id=target, device_id_type=mesh_ids)

    list_copy.start()
    for q in range(C):
        load_copy(q).start()
    smoother_copy.start()

    @pl.when(fine)
    def _():
        for p in range(NP):
            level_copy(p).start()
        for p in range(NP):
            transfer_copy(p).start()
        for q in range(C):
            load_copy(q).wait()

            def body(i):
                v = load_v[q][:, panel_at(i)]
                current[q][i] = v
                outgoing[0][q][i] = v.astype(BF)

            over_rows(body)

    @pl.when(coarse)
    def _():
        for p in range(NP):
            transfer_copy(p).start()
        for p in range(NP):
            level_copy(p).start()
        for q in range(C):
            load_copy(q).wait()
        transpose_transfer()

    list_copy.wait()
    pl.semaphore_wait(barrier, 4)

    @pl.when(fine)
    def _():
        for q in range(C):
            pair_out(0, q).start()

    for side in range(3):
        list_out(side).start()
    transpose_smoother()
    for side in range(3):
        list_out((1, 0, 2)[side]).wait_recv()

    @pl.when(fine)
    def _():
        for q in range(C):
            smooth_rows(0, q, outgoing[0][q])
            exchange(0, q)
        transpose_level()
        for q in range(C):
            exchange_wait(0, q)

            def give(i, e):
                corr[q][i] = e

            second_step(0, q, give)
        transpose_transfer()
        for q in range(C):
            pair_out(0, q).wait_recv()

            def body(i):
                x = corr[q][i] + dot(gathered(arrived[0][q], transfer_cols, i, KT), transfer_t[i])
                state[q][i] = x
                keep_step(1, q, i, x.astype(BF))

            over_rows(body)
            exchange(1, q)
        for q in range(C):
            exchange_wait(1, q)

            def body(i):
                r = load_v[q][:, panel_at(i)] - dot(gathered(ext[1][q], level_cols, i, K), level_t[i])
                current[q][i] = r
                outgoing[1][q][i] = r.astype(BF)

            over_rows(body)
            pair_out(1, q).start()
            smooth_rows(2, q, outgoing[1][q])
            exchange(2, q)
        for q in range(C):
            exchange_wait(2, q)

            def give(i, e):
                state[q][i] = state[q][i] + e

            second_step(2, q, give)
        for q in range(C):
            pair_out(1, q).wait_recv()

            def body(i):
                put(q, i, state[q][i] + dot(
                    gathered(arrived[1][q], transfer_cols, i, KT), transfer_t[i]))

            over_rows(body)
        for q in range(C):
            for side in range(3):
                ext_out(2, q, side).wait_send()

    @pl.when(coarse)
    def _():
        transpose_level()
        for t in range(2):
            for q in range(C):
                pair_out(t, q).wait_recv()
                restrict_rows(t, t, q)
                exchange(t, q)
            for q in range(C):
                exchange_wait(t, q)

                def give(i, e):
                    outgoing[t][q][i] = e.astype(BF)
                    if t == 1:
                        put(q, i, e)

                second_step(t, q, give)
                pair_out(t, q).start()

    for side in range(3):
        list_out(side).wait_send()
    for t in range(2):
        for q in range(C):
            pair_out(t, q).wait_send()
            for side in range(3):
                ext_out(t, q, side).wait_send()


def local(loads, level_blocks, level_cols, smoother, transfer_blocks, transfer_cols, bound_rows):
    vmem = pltpu.VMEM
    dma = pltpu.SemaphoreType.DMA
    any_spec = pl.BlockSpec(memory_space=pl.ANY)
    smem_spec = pl.BlockSpec(memory_space=pltpu.SMEM)

    def panels(count, kind):
        return vmem((count, M, BS), kind)

    scratch = [
        vmem((S, K, BS, BS), BF), vmem((S, KT, BS, BS), BF), vmem((S, BS, BS), BF),
        vmem((S, K * BS, BS), BF), vmem((S, KT * BS, BS), BF), vmem((S, BS, BS), BF),
        pltpu.SMEM((3, HB), jnp.int32), pltpu.SMEM((3, 3, HB), jnp.int32),
        dma((C,)), dma((NP,)), dma((NP,)), dma, dma,
        dma((3,)), dma((3,)), dma((2, C)), dma((2, C)), dma((3, C, 3)), dma((3, C, 3)),
    ]
    scratch += [vmem((M, S * BS), F32)] * C
    scratch += [panels(S, F32)] * (3 * C)
    scratch += [panels(S, BF)] * (7 * C)
    scratch += [panels(EXT, BF)] * (3 * C)
    scratch += [vmem((3, HB, M, BS), BF)] * (3 * C)
    blocks = 2 * S * (3 * K + 2 * KT + 4)
    return pl.pallas_call(
        kernel,
        out_shape=jax.ShapeDtypeStruct(loads.shape, F32),
        in_specs=[any_spec, any_spec, smem_spec, any_spec, any_spec, smem_spec, any_spec],
        out_specs=pl.BlockSpec(memory_space=vmem),
        scratch_shapes=scratch,
        cost_estimate=pl.CostEstimate(
            flops=blocks * NCOL * BS * BS, bytes_accessed=12 << 20, transcendentals=0),
        compiler_params=pltpu.CompilerParams(
            collective_id=0, has_side_effects=True, vmem_limit_bytes=48 << 20),
    )(loads, level_blocks, level_cols, smoother, transfer_blocks, transfer_cols, bound_rows)


def solution(mesh):
    in_specs = (
        P("level", None, "dom"),
        P("level", "dom", None, None, None),
        P("level", "dom", None),
        P("level", "dom", None, None),
        P("level", "dom", None, None, None),
        P("level", "dom", None),
        P("level", "dom", None, None),
    )
    out_specs = P("level", None, "dom")
    return jax.shard_map(local, mesh=mesh, in_specs=in_specs, out_specs=out_specs, check_vma=False)
```

time: 182 us -> 93.4 us (0.51)
  waiting for transfers between devices: 93.2 us -> 0 us
  Pallas kernels: 0 us -> 85.8 us
  starting transfers between devices: 24.4 us -> 0 us
  other arithmetic: 19.8 us -> 0 us
  matrix products: 19 us -> 0 us
  local copies, waits for them, and re-layouts: 24.9 us -> 7.27 us
    ppermute x14 -> x0, waiting for transfers between devices: 93.2 us -> none  [the longest x4 57.6 us: from_behind(): return lax.ppermute(x, axis, pairs)]
    pallas_call x0 -> x1, Pallas kernels: none -> 85.8 us  [local(): pl.pallas_call(kernel, out_shape=jax.ShapeDtypeStruct(loads.shape, F32),...]
    ppermute x14 -> x0, starting transfers between devices: 24.4 us -> none  [the longest x4 11.2 us: from_behind(): return lax.ppermute(x, axis, pairs)]
    dot_general x7 -> x0, matrix products: 19 us -> none  [the longest x4 13.6 us: smooth(): jnp.einsum('csb,sab->csa', panels, smoother_here, preferred_element_type=...]
    gather x10 -> x0, local copies, waits for them, and re-layouts: 15.7 us -> none  [the longest x5 12.4 us: apply_blocks(): picked = jnp.take(panels, columns.reshape(-1), axis=1)]
    select_n x12 -> x0, other arithmetic: 14 us -> none  [the longest x8 13.3 us: apply_blocks(): picked = jnp.take(panels, columns.reshape(-1), axis=1)]
    unnamed x8 -> x10, local copies, waits for them, and re-layouts: 2.62 us -> 7.27 us
    cond x6 -> x0, local copies, waits for them, and re-layouts: 2.91 us -> none
  transfers between devices with their start and end apart: 14 -> 0, of which waited for: 13 -> 0; matrix products, arithmetic and copies ran while one was open for 4% -> 0% of each run, Pallas kernels for 0% -> 0%
where the time goes in v1:
time: 93.4 us; the launch traced here: 93.1 us
  Pallas kernels  85.8 us (92%)
  local copies, waits for them, and re-layouts  7.27 us (8%)
    pallas_call x1, Pallas kernels, local(): pl.pallas_call(kernel, out_shape=jax.ShapeDtypeStruct(loads.shape, F32),...  85.8 us
    unnamed x10, local copies, waits for them, and re-layouts  7.27 us

profile of v1, /device:TPU:64, one launch (start us, length us, event | category | flops | bytes accessed | tf_op | source)
XLA Modules:
  0.0 93.1 jit_solution(3581605698283928190)
XLA Ops:
  0.0 0.7 copy.10.bounds
  0.7 0.8 copy.8.level_cols
  1.4 0.8 copy.9.transfer_cols
  2.2 0.0 copy-start
  2.2 2.2 %copy-done = bf16[1,16,8,128,128]{4,3,2,1,0:T(8,128)(2,1)S(1)} copy-done((bf16[1,16,8,128,128]{4,3,2,1,0:T(8,128)(2,1)S(1)}, bf16[1,16,8,128,128]{4,3,2,1,0:T(8,128)(2,1)}, u32[]{:S(2)}) %copy-start) | copy-done | bytes 4194328
  4.4 0.0 copy-start.1
  4.4 1.0 %copy-done.1 = f32[1,64,2048]{2,1,0:T(8,128)S(1)} copy-done((f32[1,64,2048]{2,1,0:T(8,128)S(1)}, f32[1,64,2048]{2,1,0:T(8,128)}, u32[]{:S(2)}) %copy-start.1) | copy-done | bytes 524312
  5.4 0.0 copy-start.2
  5.4 1.0 %copy-done.2 = bf16[1,16,128,128]{3,2,1,0:T(8,128)(2,1)S(1)} copy-done((bf16[1,16,128,128]{3,2,1,0:T(8,128)(2,1)S(1)}, bf16[1,16,128,128]{3,2,1,0:T(8,128)(2,1)}, u32[]{:S(2)}) %copy-start.2) | copy-done | bytes 524312
  6.5 85.8 %shard_map.73 = f32[1,64,2048]{2,1,0:T(8,128)S(1)} custom-call(f32[1,64,2048]{2,1,0:T(8,128)S(1)} %copy-done.1, bf16[1,16,12,128,128]{4,3,2,1,0:T(8,128)(2,1)} %level.1, s32[1,16,12]{2,1,0:T(8,128)S(1)} %copy.8.level_cols, bf16[1,16,128,128]{3,2,1,0:T(8,128)(2,1)S(1)} %copy-done.2, bf16[1,16,8,128,128]{4,3,2,1,0:T(8,128)(2,1)S(1)} %copy-done, ...), custom_call_target="tpu_custom_call" | custom-call | flops 1879048192 | bytes 12582912 | tf_op jit(solution)/shard_map/pallas_call | solution.py:347
  92.3 0.8 copy.12
Async XLA Ops:
  2.2 2.2 %copy-start = (bf16[1,16,8,128,128]{4,3,2,1,0:T(8,128)(2,1)S(1)}, bf16[1,16,8,128,128]{4,3,2,1,0:T(8,128)(2,1)}, u32[]{:S(2)}) copy-start(bf16[1,16,8,128,128]{4,3,2,1,0:T(8,128)(2,1)} %transfer.1) | copy-start | bytes 12582916
  4.4 1.0 %copy-start.1 = (f32[1,64,2048]{2,1,0:T(8,128)S(1)}, f32[1,64,2048]{2,1,0:T(8,128)}, u32[]{:S(2)}) copy-start(f32[1,64,2048]{2,1,0:T(8,128)} %loads.1) | copy-start | bytes 1572868
  5.4 1.0 %copy-start.2 = (bf16[1,16,128,128]{3,2,1,0:T(8,128)(2,1)S(1)}, bf16[1,16,128,128]{3,2,1,0:T(8,128)(2,1)}, u32[]{:S(2)}) copy-start(bf16[1,16,128,128]{3,2,1,0:T(8,128)(2,1)} %smoother.1) | copy-start | bytes 1572868

commit v2 on v1

--- a/solution.py
+++ b/solution.py
@@ -13,9 +13,10 @@
 KT = 8
 HB = 4
 NCOL = 64
-C = 2
-M = NCOL // C
-U = 4
+SIZES = (16, 16, 16, 16)
+C = len(SIZES)
+BEGIN = [sum(SIZES[:q]) for q in range(C)]
+U = 8
 PIECE = 4
 NP = S // PIECE
 EXT = S + 3 * HB
@@ -29,7 +30,7 @@
 
 
 def gathered(ref, cols_ref, i, count):
-    return jnp.concatenate([ref[cols_ref[0, i, k]] for k in range(count)], axis=1)
+    return jnp.concatenate([ref[cols_ref(i, k)] for k in range(count)], axis=1)
 
 
 def over_rows(body, step=U):
@@ -46,25 +47,34 @@
 
 
 def kernel(
-    loads, level, level_cols, smoother, transfer, transfer_cols, bounds, out,
+    loads, level, level_cols_in, smoother, transfer, transfer_cols_in, bounds, out,
+    level_cols, transfer_cols,
     level_raw, transfer_raw, smoother_raw, level_t, transfer_t, smoother_t,
     lists, wants,
-    load_sem, level_sem, transfer_sem, smoother_sem, list_sem,
+    load_sem, level_sem, transfer_sem, smoother_sem, list_sem, cols_sem, result_sem,
     list_send, list_recv, pair_send, pair_recv, ext_send, ext_recv,
     *refs,
 ):
     refs = list(refs)
 
+    def level_col(i, k):
+        return level_cols[k, 0, i]
+
+    def transfer_col(i, k):
+        return transfer_cols[0, k, i]
+
     def take(*dims):
         if not dims:
             return refs.pop(0)
         return [take(*dims[1:]) for _ in range(dims[0])]
 
     load_v = take(C)
+    result = take(C)
     current = take(C)
     corr = take(C)
     state = take(C)
     outgoing = take(2, C)
+    rounded = take(C)
     arrived = take(2, C)
     own = take(3, C)
     ext = take(3, C)
@@ -82,7 +92,7 @@
     mesh_ids = pl.DeviceIdType.MESH
 
     def load_copy(q):
-        return pltpu.make_async_copy(loads.at[0, pl.ds(q * M, M)], load_v[q], load_sem.at[q])
+        return pltpu.make_async_copy(loads.at[0, pl.ds(BEGIN[q], SIZES[q])], load_v[q], load_sem.at[q])
 
     def level_copy(p):
         rows = pl.ds(p * PIECE, PIECE)
@@ -93,7 +103,12 @@
         return pltpu.make_async_copy(transfer.at[0, rows], transfer_raw.at[rows], transfer_sem.at[p])
 
     smoother_copy = pltpu.make_async_copy(smoother.at[0], smoother_raw, smoother_sem)
-    list_copy = pltpu.make_async_copy(bounds.at[0, 0], lists, list_sem)
+    list_copy = pltpu.make_async_copy(bounds.at[0, :, 0], lists, list_sem)
+
+    cols_copies = (
+        pltpu.make_async_copy(level_cols_in, level_cols, cols_sem.at[0]),
+        pltpu.make_async_copy(transfer_cols_in, transfer_cols, cols_sem.at[1]),
+    )
 
     def list_out(side):
         target, slot = ((left, 1), (right, 0), (sibling, 2))[side]
@@ -105,6 +120,9 @@
         return pltpu.make_async_remote_copy(
             src_ref=outgoing[t][q], dst_ref=arrived[t][q], send_sem=pair_send.at[t, q],
             recv_sem=pair_recv.at[t, q], device_id=pair, device_id_type=mesh_ids)
+
+    def pair_start(t, q):
+        pair_out(t, q).start()
 
     def ext_out(p, q, side):
         target, slot = ((left, 1), (right, 0), (sibling, 2))[side]
@@ -173,28 +191,39 @@
     def restrict_rows(t, p, q):
         def body(i):
             v = load_v[q][:, panel_at(i)] + dot(
-                gathered(arrived[t][q], transfer_cols, i, KT), transfer_t[i])
+                gathered(arrived[t][q], transfer_col, i, KT), transfer_t[i])
             current[q][i] = v
-            keep_step(p, q, i, dot(v.astype(BF), smoother_t[i]).astype(BF))
+            rounded[q][i] = v.astype(BF)
 
         over_rows(body)
+        smooth_rows(p, q, rounded[q])
 
     def second_step(p, q, give):
         def body(i):
-            applied = dot(gathered(ext[p][q], level_cols, i, K), level_t[i])
-            second_in = (current[q][i] - applied).astype(BF)
-            give(i, own[p][q][i].astype(F32) + dot(second_in, smoother_t[i]))
+            applied = dot(gathered(ext[p][q], level_col, i, K), level_t[i])
+            rounded[q][i] = (current[q][i] - applied).astype(BF)
 
         over_rows(body)
 
+        def finish(i):
+            give(i, own[p][q][i].astype(F32) + dot(rounded[q][i], smoother_t[i]))
+
+        over_rows(finish)
+
     def put(q, i, value):
-        out[0, q * M : (q + 1) * M, panel_at(i)] = value
+        result[q][:, panel_at(i)] = value
+
+    def result_copy(q):
+        return pltpu.make_async_copy(
+            result[q], out.at[0, pl.ds(BEGIN[q], SIZES[q])], result_sem.at[q])
 
     barrier = pltpu.get_barrier_semaphore()
     for target in (left, right, sibling, pair):
         pl.semaphore_signal(barrier, inc=1, device_id=target, device_id_type=mesh_ids)
 
     list_copy.start()
+    for copy in cols_copies:
+        copy.start()
     for q in range(C):
         load_copy(q).start()
     smoother_copy.start()
@@ -226,15 +255,18 @@
         transpose_transfer()
 
     list_copy.wait()
+    for copy in cols_copies:
+        copy.wait()
     pl.semaphore_wait(barrier, 4)
+
+    for side in range(3):
+        list_out(side).start()
 
     @pl.when(fine)
     def _():
         for q in range(C):
-            pair_out(0, q).start()
-
-    for side in range(3):
-        list_out(side).start()
+            pair_start(0, q)
+
     transpose_smoother()
     for side in range(3):
         list_out((1, 0, 2)[side]).wait_recv()
@@ -257,7 +289,7 @@
             pair_out(0, q).wait_recv()
 
             def body(i):
-                x = corr[q][i] + dot(gathered(arrived[0][q], transfer_cols, i, KT), transfer_t[i])
+                x = corr[q][i] + dot(gathered(arrived[0][q], transfer_col, i, KT), transfer_t[i])
                 state[q][i] = x
                 keep_step(1, q, i, x.astype(BF))
 
@@ -267,12 +299,13 @@
             exchange_wait(1, q)
 
             def body(i):
-                r = load_v[q][:, panel_at(i)] - dot(gathered(ext[1][q], level_cols, i, K), level_t[i])
+                r = load_v[q][:, panel_at(i)] - dot(gathered(ext[1][q], level_col, i, K), level_t[i])
                 current[q][i] = r
                 outgoing[1][q][i] = r.astype(BF)
 
             over_rows(body)
-            pair_out(1, q).start()
+            pair_start(1, q)
+        for q in range(C):
             smooth_rows(2, q, outgoing[1][q])
             exchange(2, q)
         for q in range(C):
@@ -287,9 +320,10 @@
 
             def body(i):
                 put(q, i, state[q][i] + dot(
-                    gathered(arrived[1][q], transfer_cols, i, KT), transfer_t[i]))
+                    gathered(arrived[1][q], transfer_col, i, KT), transfer_t[i]))
 
             over_rows(body)
+            result_copy(q).start()
         for q in range(C):
             for side in range(3):
                 ext_out(2, q, side).wait_send()
@@ -311,8 +345,12 @@
                         put(q, i, e)
 
                 second_step(t, q, give)
-                pair_out(t, q).start()
-
+                pair_start(t, q)
+                if t == 1:
+                    result_copy(q).start()
+
+    for q in range(C):
+        result_copy(q).wait()
     for side in range(3):
         list_out(side).wait_send()
     for t in range(2):
@@ -325,36 +363,38 @@
 def local(loads, level_blocks, level_cols, smoother, transfer_blocks, transfer_cols, bound_rows):
     vmem = pltpu.VMEM
     dma = pltpu.SemaphoreType.DMA
-    any_spec = pl.BlockSpec(memory_space=pl.ANY)
-    smem_spec = pl.BlockSpec(memory_space=pltpu.SMEM)
-
-    def panels(count, kind):
-        return vmem((count, M, BS), kind)
+    any_spec = pl.BlockSpec(memory_space=pltpu.HBM)
+
+    def each(kind, *dims):
+        return [vmem(tuple(m if n is None else n for n in dims), kind) for m in SIZES]
 
     scratch = [
+        pltpu.SMEM((K, 1, S), jnp.int32), pltpu.SMEM((1, KT, S), jnp.int32),
         vmem((S, K, BS, BS), BF), vmem((S, KT, BS, BS), BF), vmem((S, BS, BS), BF),
         vmem((S, K * BS, BS), BF), vmem((S, KT * BS, BS), BF), vmem((S, BS, BS), BF),
         pltpu.SMEM((3, HB), jnp.int32), pltpu.SMEM((3, 3, HB), jnp.int32),
-        dma((C,)), dma((NP,)), dma((NP,)), dma, dma,
+        dma((C,)), dma((NP,)), dma((NP,)), dma, dma, dma((2,)), dma((C,)),
         dma((3,)), dma((3,)), dma((2, C)), dma((2, C)), dma((3, C, 3)), dma((3, C, 3)),
     ]
-    scratch += [vmem((M, S * BS), F32)] * C
-    scratch += [panels(S, F32)] * (3 * C)
-    scratch += [panels(S, BF)] * (7 * C)
-    scratch += [panels(EXT, BF)] * (3 * C)
-    scratch += [vmem((3, HB, M, BS), BF)] * (3 * C)
+    scratch += each(F32, None, S * BS) * 2
+    scratch += each(F32, S, None, BS) * 3
+    scratch += each(BF, S, None, BS) * 8
+    scratch += each(BF, EXT, None, BS) * 3
+    scratch += each(BF, 3, HB, None, BS) * 3
     blocks = 2 * S * (3 * K + 2 * KT + 4)
     return pl.pallas_call(
         kernel,
         out_shape=jax.ShapeDtypeStruct(loads.shape, F32),
-        in_specs=[any_spec, any_spec, smem_spec, any_spec, any_spec, smem_spec, any_spec],
-        out_specs=pl.BlockSpec(memory_space=vmem),
+        in_specs=[any_spec] * 7,
+        out_specs=any_spec,
         scratch_shapes=scratch,
         cost_estimate=pl.CostEstimate(
             flops=blocks * NCOL * BS * BS, bytes_accessed=12 << 20, transcendentals=0),
         compiler_params=pltpu.CompilerParams(
-            collective_id=0, has_side_effects=True, vmem_limit_bytes=48 << 20),
-    )(loads, level_blocks, level_cols, smoother, transfer_blocks, transfer_cols, bound_rows)
+            collective_id=0, has_side_effects=True, vmem_limit_bytes=64 << 20),
+    )(
+        loads, level_blocks, jnp.transpose(level_cols, (2, 0, 1)), smoother, transfer_blocks,
+        jnp.transpose(transfer_cols, (0, 2, 1)), jnp.transpose(bound_rows, (0, 2, 1, 3)))
 
 
 def solution(mesh):

time: 93.4 us -> 75.9 us (0.81)
  Pallas kernels: 85.8 us -> 73.9 us
  local copies, waits for them, and re-layouts: 7.27 us -> 1.87 us
    pallas_call x1, Pallas kernels: 85.8 us -> 73.9 us  [local(): pl.pallas_call(kernel, out_shape=jax.ShapeDtypeStruct(loads.shape, F32),...]
    unnamed x10 -> x1, local copies, waits for them, and re-layouts: 7.27 us -> 1.87 us
where the time goes in v2:
time: 75.9 us; the launch traced here: 75.8 us
  Pallas kernels  73.9 us (97%)
  local copies, waits for them, and re-layouts  1.87 us (2%)
    pallas_call x1, Pallas kernels, local(): pl.pallas_call(kernel, out_shape=jax.ShapeDtypeStruct(loads.shape, F32),...  73.9 us
    unnamed x1, local copies, waits for them, and re-layouts  1.87 us

profile of v2, /device:TPU:64, one launch (start us, length us, event | category | flops | bytes accessed | tf_op | source)
XLA Modules:
  0.0 75.8 jit_solution(11352351864462785896)
XLA Ops:
  0.0 73.9 %shard_map.73 = f32[1,64,2048]{2,1,0:T(8,128)} custom-call(f32[1,64,2048]{2,1,0:T(8,128)} %loads.1, bf16[1,16,12,128,128]{4,3,2,1,0:T(8,128)(2,1)} %level.1, s32[12,1,16]{2,1,0:T(1,128)} %bitcast.3, bf16[1,16,128,128]{3,2,1,0:T(8,128)(2,1)} %smoother.1, bf16[1,16,8,128,128]{4,3,2,1,0:T(8,128)(2,1)} %transfer.1, s32[1,8,16]{2,1,0:T(8,128)} %bitcast.4, ...), custom_call_target="tpu_custom_call" | custom-call | flops 1879048192 | bytes 12582912 | tf_op jit(solution)/shard_map/pallas_call | solution.py:385
  73.9 1.9 %copy.9 = f32[1,64,2048]{2,1,0:T(8,128)} copy(f32[1,64,2048]{2,1,0:T(8,128)} %shard_map.73) | data formatting | bytes 1048576

commit v3 on v2

--- a/solution.py
+++ b/solution.py
@@ -172,11 +172,10 @@
     def transpose_smoother():
         smoother_copy.wait()
 
-        def body(i, carry):
+        def body(i):
             smoother_t[i] = smoother_raw[i].T
-            return carry
-
-        lax.fori_loop(0, S, body, 0)
+
+        over_rows(body)
 
     def keep_step(p, q, i, first):
         own[p][q][i] = first
@@ -268,15 +267,18 @@
             pair_start(0, q)
 
     transpose_smoother()
-    for side in range(3):
-        list_out((1, 0, 2)[side]).wait_recv()
+    transpose_level()
+
+    def lists_wait():
+        for side in range(3):
+            list_out((1, 0, 2)[side]).wait_recv()
 
     @pl.when(fine)
     def _():
+        lists_wait()
         for q in range(C):
             smooth_rows(0, q, outgoing[0][q])
             exchange(0, q)
-        transpose_level()
         for q in range(C):
             exchange_wait(0, q)
 
@@ -330,11 +332,12 @@
 
     @pl.when(coarse)
     def _():
-        transpose_level()
         for t in range(2):
             for q in range(C):
                 pair_out(t, q).wait_recv()
                 restrict_rows(t, t, q)
+                if t == 0 and q == 0:
+                    lists_wait()
                 exchange(t, q)
             for q in range(C):
                 exchange_wait(t, q)
@@ -391,10 +394,10 @@
         cost_estimate=pl.CostEstimate(
             flops=blocks * NCOL * BS * BS, bytes_accessed=12 << 20, transcendentals=0),
         compiler_params=pltpu.CompilerParams(
-            collective_id=0, has_side_effects=True, vmem_limit_bytes=64 << 20),
-    )(
+            collective_id=0, has_side_effects=True, vmem_limit_bytes=48 << 20),
+    )(*(pltpu.with_memory_space_constraint(a, pltpu.HBM) for a in (
         loads, level_blocks, jnp.transpose(level_cols, (2, 0, 1)), smoother, transfer_blocks,
-        jnp.transpose(transfer_cols, (0, 2, 1)), jnp.transpose(bound_rows, (0, 2, 1, 3)))
+        jnp.transpose(transfer_cols, (0, 2, 1)), jnp.transpose(bound_rows, (0, 2, 1, 3)))))
 
 
 def solution(mesh):

time: 75.9 us -> 74.4 us (0.980)
  local copies, waits for them, and re-layouts: 1.87 us -> 0.8 us
    unnamed x1, local copies, waits for them, and re-layouts: 1.87 us -> 0.8 us
where the time goes in v3:
time: 74.4 us
  Pallas kernels  73.6 us (99%)
  local copies, waits for them, and re-layouts  0.8 us (1%)
    pallas_call x1, Pallas kernels, local(): pl.pallas_call(kernel, out_shape=jax.ShapeDtypeStruct(loads.shape, F32),...  73.6 us

profile of v3, /device:TPU:64, one launch (start us, length us, event | category | flops | bytes accessed | tf_op | source)
XLA Modules:
  0.0 74.4 jit_solution(14780990243465265768)
XLA Ops:
  0.0 73.6 %shard_map.73 = f32[1,64,2048]{2,1,0:T(8,128)S(1)} custom-call(f32[1,64,2048]{2,1,0:T(8,128)} %loads.1, bf16[1,16,12,128,128]{4,3,2,1,0:T(8,128)(2,1)} %level.1, s32[12,1,16]{2,1,0:T(1,128)} %bitcast.3, bf16[1,16,128,128]{3,2,1,0:T(8,128)(2,1)} %smoother.1, bf16[1,16,8,128,128]{4,3,2,1,0:T(8,128)(2,1)} %transfer.1, s32[1,8,16]{2,1,0:T(8,128)} %bitcast.4, ...), custom_call_target="tpu_custom_call" | custom-call | flops 1879048192 | bytes 12582912 | tf_op jit(solution)/shard_map/pallas_call | solution.py:388
  73.6 0.8 %copy.9 = f32[1,64,2048]{2,1,0:T(8,128)} copy(f32[1,64,2048]{2,1,0:T(8,128)S(1)} %shard_map.73) | data formatting | bytes 1048576

commit v4 on v3

--- a/solution.py
+++ b/solution.py
@@ -16,7 +16,7 @@
 SIZES = (16, 16, 16, 16)
 C = len(SIZES)
 BEGIN = [sum(SIZES[:q]) for q in range(C)]
-U = 8
+U = 16
 PIECE = 4
 NP = S // PIECE
 EXT = S + 3 * HB

time: 74.4 us -> 72.4 us (0.973)
  Pallas kernels: 73.6 us -> 71.4 us
    pallas_call x1, Pallas kernels: 73.6 us -> 71.4 us  [local(): pl.pallas_call(kernel, out_shape=jax.ShapeDtypeStruct(loads.shape, F32),...]
where the time goes in v4:
time: 72.4 us; the launch traced here: 72.2 us
  Pallas kernels  71.4 us (99%)
  local copies, waits for them, and re-layouts  0.8 us (1%)
    pallas_call x1, Pallas kernels, local(): pl.pallas_call(kernel, out_shape=jax.ShapeDtypeStruct(loads.shape, F32),...  71.4 us

profile of v4, /device:TPU:64, one launch (start us, length us, event | category | flops | bytes accessed | tf_op | source)
XLA Modules:
  0.0 72.2 jit_solution(8029228762109322808)
XLA Ops:
  0.0 71.4 %shard_map.73 = f32[1,64,2048]{2,1,0:T(8,128)S(1)} custom-call(f32[1,64,2048]{2,1,0:T(8,128)} %loads.1, bf16[1,16,12,128,128]{4,3,2,1,0:T(8,128)(2,1)} %level.1, s32[12,1,16]{2,1,0:T(1,128)} %bitcast.3, bf16[1,16,128,128]{3,2,1,0:T(8,128)(2,1)} %smoother.1, bf16[1,16,8,128,128]{4,3,2,1,0:T(8,128)(2,1)} %transfer.1, s32[1,8,16]{2,1,0:T(8,128)} %bitcast.4, ...), custom_call_target="tpu_custom_call" | custom-call | flops 1879048192 | bytes 12582912 | tf_op jit(solution)/shard_map/pallas_call | solution.py:388
  71.4 0.8 %copy.9 = f32[1,64,2048]{2,1,0:T(8,128)} copy(f32[1,64,2048]{2,1,0:T(8,128)S(1)} %shard_map.73) | data formatting | bytes 1048576
